TPU v7x, 128 devices: a whole 4x4x4 slice. The times are simulated.
128 devices in a mesh: grp: 4 (over z), dev: 32 (over y, x, core).
Axes of the slice: x: 4, y: 4, z: 4, core: 2. Of those that a mesh axis runs over, the one named last changes fastest.
Arguments:
- coef: bfloat16 [2048, 393216], P('dev', 'grp'), may hold values from -6 to 6
- basis_idx: int32 [64, 512], replicated, may hold values from 0 to 255
- basis_w: float32 [64, 8, 512], replicated, may hold values from -0.25 to 0.25
- owner_blocks: int32 [256], replicated, may hold values from 0 to 255, each once
- data: float32 [393216], P(('grp', 'dev')), may hold values from -6 to 6
- panel_live: int32 [128], P(('grp', 'dev')), may hold values from 2304 to 3072, as said below
Outputs:
- r_factor: float32 [512, 512], replicated
- projected: float32 [512], replicated
- q_rows: float32 [393216, 512], P(('grp', 'dev'))
Inputs may be any that keep to these rules, and one draw needn't show every extreme that they name: `owner_blocks`: each block index appears once. `panel_live`: some panel is full in every draw.
All inputs are finite; a program needn't handle non-finite values.
Results may differ from a plain program's by a relative error of at most 0.0038.
Values may be sent and summed in bfloat16 or wider, within the bound.
A program may use at most 128 MiB of HBM per device.

v0:
```python
import jax
import jax.numpy as jnp
from jax import lax
from jax.sharding import PartitionSpec as P


def build_basis(basis_idx, basis_w, owner_blocks):
    one_hot = (basis_idx[:, None, :] == owner_blocks[None, :, None]).astype(jnp.float32)
    dense_basis = jnp.einsum("tbk,tdk->bdk", one_hot, basis_w, precision=lax.Precision.HIGHEST)
    return dense_basis.reshape(-1, dense_basis.shape[2]).astype(jnp.bfloat16)


def cross_gram(left, right):
    return jnp.dot(left.T, right, precision=lax.Precision.HIGHEST)


def on_device(coef, basis_idx, basis_w, owner_blocks, data, panel_live):
    panel_coef = lax.all_to_all(coef, "dev", split_axis=1, concat_axis=0, tiled=True)
    dense_basis = build_basis(basis_idx, basis_w, owner_blocks)
    green_rows = lax.dot_general(
        panel_coef, dense_basis, (((0,), (0,)), ((), ())), preferred_element_type=jnp.float32
    )
    row_index = jnp.arange(green_rows.shape[0], dtype=jnp.int32)
    row_mask = row_index < panel_live[0]
    green_rows = jnp.where(row_mask[:, None], green_rows, jnp.float32(0.0))
    live_data = jnp.where(row_mask, data, jnp.float32(0.0))
    gram_local = cross_gram(green_rows, green_rows)
    rhs_local = jnp.dot(live_data, green_rows, precision=lax.Precision.HIGHEST)
    gram_group, rhs_group = lax.psum((gram_local, rhs_local), "dev")
    gram_total, rhs_total = lax.psum((gram_group, rhs_group), "grp")
    lower_factor = jnp.linalg.cholesky(gram_total)
    projected = jax.scipy.linalg.solve_triangular(lower_factor, rhs_total, lower=True)
    rows_total = green_rows.shape[0] * lax.axis_size("dev") * lax.axis_size("grp")
    r_factor = lower_factor.T / jnp.sqrt(jnp.float32(rows_total))
    q_rows = jax.scipy.linalg.solve_triangular(r_factor.T, green_rows.T, lower=True).T
    return (r_factor, projected, q_rows)


def solution(mesh):
    in_specs = (P("dev", "grp"), P(), P(), P(), P(("grp", "dev")), P(("grp", "dev")))
    out_specs = (P(), P(), P(("grp", "dev"), None))
    return jax.shard_map(
        on_device, mesh=mesh, in_specs=in_specs, out_specs=out_specs, check_vma=False
    )
```

profile of v0, /device:TPU:0, one launch (start us, length us, event | category | flops | bytes accessed | tf_op | source)
XLA Modules:
  0.0 634.4 jit_solution(3695777452856139123)
XLA Ops:
  7.2 10.9 %copy.41 = bf16[8,32,8,3072]{3,2,0,1:T(8,128)(2,1)} copy(bf16[8,32,8,3072]{3,2,1,0:T(8,128)(2,1)} %bitcast.148) | data formatting | bytes 25165824 | tf_op jit(solution)/shard_map/all_to_all | solution.py:18
  18.1 7.7 %all-to-all-start = ((bf16[64,32,3072]{2,0,1:T(8,128)(2,1)}), bf16[64,32,3072]{2,0,1:T(8,128)(2,1)}, u32[]{:S(2)}, u32[]{:S(2)}) async-start(bf16[64,32,3072]{2,0,1:T(8,128)(2,1)} %bitcast.147), calls=%async_computation | async-start | bytes 25165824 | tf_op jit(solution)/shard_map/all_to_all | solution.py:18
  26.5 1.1 copy.31
  27.8 13.4 %convert_bitcast_fusion = bf16[256,8,512]{0,1,2:T(8,128)(2,1)} fusion(f32[64,8,512]{0,1,2:T(8,128)S(1)} %copy.31, s32[256]{0:T(256)S(1)} %copy-done.6, s32[64,512]{0,1:T(8,128)S(1)} %copy.30), kind=kOutput, calls=%fused_computation.26 | convolution fusion | flops 814743552 | bytes 3277824 | tf_op jit(solution)/shard_map/tbk,tdk->bdk/dot_general | solution.py:9
  41.2 3.8 copy.32
  45.0 141.1 %all-to-all-done = bf16[64,32,3072]{2,0,1:T(8,128)(2,1)} async-done(((bf16[64,32,3072]{2,0,1:T(8,128)(2,1)}), bf16[64,32,3072]{2,0,1:T(8,128)(2,1)}, u32[]{:S(2)}, u32[]{:S(2)}) %all-to-all-start) | async-done | bytes 12582944 | tf_op jit(solution)/shard_map/all_to_all | solution.py:18
  186.1 9.3 %convolution_select_fusion = f32[512,3072]{1,0:T(8,128)S(1)} fusion(bf16[2048,3072]{1,0:T(8,128)(2,1)} %bitcast.4, pred[3072]{0:T(1024)(128)(4,1)S(1)} %iota_compare_fusion.3, bf16[256,8,512]{2,1,0:T(8,128)(2,1)S(1)} %copy.32), kind=kOutput, calls=%fused_computation.18 | convolution fusion | flops 6444023808 | bytes 20974592 | tf_op jit(solution)/shard_map/dot_general | solution.py:20
  195.4 2.7 copy-done
  198.1 11.4 %fusion.68 = f32[512,512]{0,1:T(8,128)} fusion(f32[512,3072]{1,0:T(8,128)S(1)} %convolution_select_fusion), kind=kOutput, calls=%fused_computation.119 | convolution fusion | flops 9663676416 | bytes 7340032 | tf_op jit(solution)/shard_map/dot_general | solution.py:14
  209.6 103.2 %all-reduce.4.cloned.1.call-done = f32[512,512]{0,1:T(8,128)} async-done(((f32[512,512]{0,1:T(8,128)}), f32[512,512]{0,1:T(8,128)}) %all-reduce.4.cloned.1.call-update) | async-done | bytes 1048592 | tf_op jit(solution)/shard_map/psum | solution.py:29
  312.8 7.2 %fusion.4 = f32[1,512]{1,0:T(1,128)S(1)} fusion(f32[3072,1]{0,1:T(1,128)S(1)} %bitcast.149, f32[512,3072]{1,0:T(8,128)} %copy-done), kind=kOutput, calls=%fused_computation.10 | convolution fusion | flops 18874368 | bytes 6305792 | tf_op jit(solution)/shard_map/dot_general | solution.py:28
  320.0 66.2 %psum.30 = f32[512]{0:T(512)S(1)} all-reduce(f32[512]{0:T(512)S(1)} %bitcast.150), channel_id=1, replica_groups=mesh['grp'=4,'dev'=32] {'dev'}, use_global_device_ids=true, to_apply=%region_10.11 | all-reduce | flops 512 | bytes 4096 | tf_op jit(solution)/shard_map/psum | solution.py:29
  386.2 10.9 %psum.31 = f32[512]{0:T(512)S(1)} all-reduce(f32[512]{0:T(512)S(1)} %psum.30), channel_id=1, replica_groups=mesh['grp'=4,'dev'=32] {'grp'}, use_global_device_ids=true, to_apply=%region_11.12 | all-reduce | flops 512 | bytes 4096 | tf_op jit(solution)/shard_map/psum | solution.py:30
  397.1 1.6 copy.35
  399.1 11.7 %cholesky.104 = f32[128,128]{1,0:T(8,128)S(1)} custom-call(f32[128,128]{1,0:T(8,128)S(1)} %cholesky.266), custom_call_target="Cholesky" | custom-call | tf_op jit(solution)/shard_map/jit(cholesky)/cholesky | solution.py:31
  410.9 9.8 %custom-call.35 = f32[1,128,128]{1,2,0:T(8,128)S(1)} custom-call(f32[1,128,128]{2,1,0:T(8,128)S(1)} %get-tuple-element.63), custom_call_target="InvertDiagBlocksLowerTriangular" | custom-call | tf_op jit(solution)/shard_map/jit(cholesky)/cholesky | solution.py:31
  420.7 0.3 constant_dynamic-update-slice_fusion.3
  421.1 0.3 convolution_subtract_fusion.2
  421.4 11.7 %cholesky.217 = f32[128,128]{1,0:T(8,128)S(1)} custom-call(f32[128,128]{1,0:T(8,128)S(1)} %cholesky.270), custom_call_target="Cholesky" | custom-call | tf_op jit(solution)/shard_map/jit(cholesky)/cholesky | solution.py:31
  433.2 22.1 %custom-call.36 = f32[1,128,128]{1,2,0:T(8,128)S(1)} custom-call(f32[1,128,128]{2,1,0:T(8,128)S(1)} %get-tuple-element.60), custom_call_target="InvertDiagBlocksLowerTriangular" | custom-call | tf_op jit(solution)/shard_map/jit(cholesky)/cholesky | solution.py:31
  455.5 0.4 convolution_subtract_fusion.3
  455.9 11.7 %cholesky.238 = f32[128,128]{1,0:T(8,128)S(1)} custom-call(f32[128,128]{1,0:T(8,128)S(1)} %cholesky.275), custom_call_target="Cholesky" | custom-call | tf_op jit(solution)/shard_map/jit(cholesky)/cholesky | solution.py:31
  467.7 9.8 %custom-call.37 = f32[1,128,128]{1,2,0:T(8,128)S(1)} custom-call(f32[1,128,128]{2,1,0:T(8,128)S(1)} %get-tuple-element.57), custom_call_target="InvertDiagBlocksLowerTriangular" | custom-call | tf_op jit(solution)/shard_map/jit(cholesky)/cholesky | solution.py:31
  477.7 0.4 convolution_subtract_fusion.4
  478.1 11.7 %cholesky.255 = f32[128,128]{1,0:T(8,128)S(1)} custom-call(f32[128,128]{1,0:T(8,128)S(1)} %convolution_subtract_fusion.4), custom_call_target="Cholesky" | custom-call | tf_op jit(solution)/shard_map/jit(cholesky)/cholesky | solution.py:31
  489.8 0.7 compare_reduce_fusion.1
  490.6 0.6 compare_reduce_fusion
  491.2 0.6 compare_reduce_fusion.2
  494.4 1.4 fusion.30
  495.8 1.3 copy.36
  497.1 12.0 %while.2 = (s32[]{:T(128)}, f32[512,512]{1,0:T(8,128)}, s32[4,2]{0,1:T(2,128)S(1)}, f32[4,128,128]{2,1,0:T(8,128)S(1)}, s32[]{:T(128)}) while((s32[]{:T(128)}, f32[512,512]{1,0:T(8,128)}, s32[4,2]{0,1:T(2,128)S(1)}, f32[4,128,128]{2,1,0:T(8,128)S(1)}, s32[]{:T(128)}) %tuple.51), condition=%wide.while_cond, body=%wide.while_body.sunk | while | flops 2 | bytes 131189 | solution.py:32
  497.2 0.6 fusion.85
  497.8 2.3 bitcast_dynamic-update-slice_fusion.4
  500.2 0.6 fusion.85
  500.8 2.3 bitcast_dynamic-update-slice_fusion.4
  503.2 0.6 fusion.85
  503.8 2.3 bitcast_dynamic-update-slice_fusion.4
  506.3 0.6 fusion.85
  506.9 2.3 bitcast_dynamic-update-slice_fusion.4
  509.1 39.3 %custom-call.38 = f32[4,128,128]{1,2,0:T(8,128)S(1)} custom-call(f32[4,128,128]{2,1,0:T(8,128)S(1)} %get-tuple-element.10), custom_call_target="InvertDiagBlocksLowerTriangular" | custom-call | tf_op jit(solution)/shard_map/jit(_solve_triangular)/triangular_solve | solution.py:32
  548.6 1.0 fusion.25
  549.8 1.1 fusion.26
  551.1 1.2 fusion.28
  552.6 0.6 pad_maximum_fusion
  553.2 8.1 %while.3 = (s32[]{:T(128)}, f32[512,512]{1,0:T(8,128)S(1)}, s32[4,2]{0,1:T(2,128)S(1)}, f32[4,128,128]{2,1,0:T(8,128)S(1)}, s32[]{:T(128)}) while((s32[]{:T(128)}, f32[512,512]{1,0:T(8,128)S(1)}, s32[4,2]{0,1:T(2,128)S(1)}, f32[4,128,128]{2,1,0:T(8,128)S(1)}, s32[]{:T(128)}) %tuple.61), condition=%wide.while_cond.1, body=%wide.while_body.1.sunk | while | flops 2 | bytes 131189 | solution.py:35
  553.3 0.6 fusion.86
  553.9 1.3 bitcast_dynamic-update-slice_fusion.5
  555.3 0.6 fusion.86
  555.9 1.3 bitcast_dynamic-update-slice_fusion.5
  557.4 0.6 fusion.86
  558.0 1.3 bitcast_dynamic-update-slice_fusion.5
  559.4 0.6 fusion.86
  560.0 1.3 bitcast_dynamic-update-slice_fusion.5
  561.4 0.7 copy-done.3
  562.1 40.3 %custom-call.39 = f32[4,128,128]{1,2,0:T(8,128)S(1)} custom-call(f32[4,128,128]{2,1,0:T(8,128)} %copy-done.3), custom_call_target="InvertDiagBlocksLowerTriangular" | custom-call | tf_op jit(solution)/shard_map/jit(_solve_triangular)/triangular_solve | solution.py:35
  602.4 2.9 fusion.21
  605.3 3.1 convolution_subtract_fusion
  608.3 1.5 fusion.45
  609.9 1.9 convolution_subtract_fusion.1
  611.8 1.5 fusion.43
  613.2 2.9 fusion.12
  616.2 1.5 fusion.42
  617.7 3.0 maximum_bitcast_fusion
  620.6 6.6 %copy.37 = f32[3072,512]{1,0:T(8,128)} copy(f32[3072,512]{0,1:T(8,128)} %maximum_bitcast_fusion) | data formatting | bytes 12582912
  (52 shorter events, 2.7 us)
Async XLA Ops:
  18.1 8.4 %copy-start.2 = (f32[64,8,512]{2,1,0:T(8,128)S(1)}, f32[64,8,512]{2,1,0:T(8,128)}, u32[]{:S(2)}) copy-start(f32[64,8,512]{2,1,0:T(8,128)} %param.8) | copy-start | bytes 3145732
  18.1 168.0 %all-to-all-start = ((bf16[64,32,3072]{2,0,1:T(8,128)(2,1)}), bf16[64,32,3072]{2,0,1:T(8,128)(2,1)}, u32[]{:S(2)}, u32[]{:S(2)}) async-start(bf16[64,32,3072]{2,0,1:T(8,128)(2,1)} %bitcast.147), calls=%async_computation | async-start | bytes 25165824 | tf_op jit(solution)/shard_map/all_to_all | solution.py:18
  25.7 1.9 copy-start.4
  25.8 2.0 copy-start.6
  25.8 287.0 %all-reduce.4.cloned.1.call-start = ((), (), s32[]{:S(2)}) async-start(), calls=%async_computation.1 | async-start | bytes 2097152 | tf_op jit(solution)/shard_map/psum | solution.py:29
  195.4 2.7 copy-start
  209.5 103.3 %copy-start.5 = (f32[3072]{0:T(1024)S(1)}, f32[3072]{0:T(1024)}, u32[]{:S(2)}) copy-start(f32[3072]{0:T(1024)} %param.10) | copy-start | bytes 36868
  209.5 187.6 %all-reduce.6.cloned.1.call-start = ((), (), s32[]{:S(2)}) async-start(), calls=%async_computation.2 | async-start | bytes 2097152 | tf_op jit(solution)/shard_map/psum | solution.py:30
  397.1 1.7 copy-start.1
  553.2 56.6 %slice-start = ((s8[6291456]{0:T(1024)(128)(4,1)}), s8[2097152]{0:T(1024)(128)(4,1)S(1)}, s32[]{:S(2)}) async-start(s8[6291456]{0:T(1024)(128)(4,1)} %bitcast.145), calls=%async_computation.3 | async-start | bytes 4194304
  561.4 0.7 copy-start.3
  605.3 4.6 slice-start.1
Sparse Core Ops, SparseCore 0:
  209.7 103.0 all-reduce.3
  315.1 46.0 all-reduce.5
where the time goes:
time: 644 us; the launch traced here: 634 us
  waiting for transfers between devices  244 us (38%)
  other arithmetic  176 us (27%)
  blocking collectives  77.1 us (12%)
  matrix products  62.4 us (10%)
  local copies, waits for them, and re-layouts  49.1 us (8%)
  between operations  18 us (3%)
  starting transfers between devices  7.76 us (1%)
    all_to_all x1, waiting for transfers between devices, on_device(): lax.all_to_all(coef, 'dev', split_axis=1, concat_axis=0, tiled=True)  141 us
    psum x1, waiting for transfers between devices, on_device(): gram_group, rhs_group = lax.psum((gram_local, rhs_local), 'dev')  103 us
    another operation x14, other arithmetic, on_device(): lower_factor = jnp.linalg.cholesky(gram_total)  90.7 us
    psum x1, blocking collectives, on_device(): gram_group, rhs_group = lax.psum((gram_local, rhs_local), 'dev')  66.2 us
    another operation x2, other arithmetic, on_device(): jax.scipy.linalg.solve_triangular(r_factor.T, green_rows.T, lower=True)  41.7 us
    another operation x3, other arithmetic, on_device(): jax.scipy.linalg.solve_triangular(lower_factor, rhs_total, lower=True)  39.9 us
    another operation x24, local copies, waits for them, and re-layouts  20 us
    another operation x7, matrix products, on_device(): jax.scipy.linalg.solve_triangular(r_factor.T, green_rows.T, lower=True)  15.2 us
  transfers between devices with their start and end apart: 3, of which 2 were waited for; matrix products, arithmetic and copies ran while one was open for 4% of the time, Pallas kernels for 0%

commit v1 on v0

v1 whole, which is shorter than its diff:
```python
import functools

import jax
import jax.numpy as jnp
from jax import lax
from jax.experimental import pallas as pl
from jax.experimental.pallas import tpu as pltpu
from jax.sharding import PartitionSpec as P

HI = lax.Precision.HIGHEST
MESH = pl.DeviceIdType.MESH
NB = 128
SB = 8
CHUNK = 256
BLK = 8
NY, NX, NC, NZ = 4, 4, 2, 4
NCHIP = NY * NX
NDEV = NCHIP * NC
PIECE = 48
HALF = NCHIP * PIECE


def hops(oy, ox):
    return min(oy, NY - oy) + min(ox, NX - ox)


def peer_offsets():
    offs = [(oy, ox, oc) for oy in range(NY) for ox in range(NX) for oc in range(NC)]
    return sorted(offs[1:], key=lambda o: hops(o[0], o[1]))


def chip_offsets():
    offs = [(oy, ox) for oy in range(NY) for ox in range(NX)][1:]
    return sorted(offs, key=lambda o: -hops(o[0], o[1]))


def upper_blocks(k):
    n = k // NB
    return [(p, q) for p in range(n) for q in range(p, n)]


def dot_t(a, b):
    return lax.dot_general(a, b, (((0,), (0,)), ((), ())), preferred_element_type=jnp.float32)


def split(x):
    high = x.astype(jnp.bfloat16)
    return high, (x - high.astype(jnp.float32)).astype(jnp.bfloat16)


def green_kernel(
    owner_ref, live_ref, coef_ref, idx_ref, w_ref, data_ref,
    green_ref, sum_ref,
    panel, basis, gbuf, gram, rhs, packed, half, from_core, from_chip, from_z, total,
    send_a, recv_a, local_a, out_g, send_c, recv_c, send_p, recv_p, send_z, recv_z, send_g, recv_g, send_f, recv_f,
):
    rows = green_ref.shape[0]
    k = green_ref.shape[1]
    depth = coef_ref.shape[0]
    chunks = rows // CHUNK
    z, me = lax.axis_index("grp"), lax.axis_index("dev")
    c, x, y = me % NC, (me // NC) % NX, me // (NC * NX)
    chip = y * NX + x
    partner = chip * NC + (1 - c)
    peers = peer_offsets()
    chips = chip_offsets()

    def device_at(oy, ox, oc):
        return (lax.rem(y + oy, NY) * NX + lax.rem(x + ox, NX)) * NC + lax.rem(c + oc, NC)

    barrier = pltpu.get_barrier_semaphore()
    for off in peers:
        pl.semaphore_signal(barrier, inc=1, device_id=(z, device_at(*off)), device_id_type=MESH)
    for oz in range(1, NZ):
        pl.semaphore_signal(barrier, inc=1, device_id=(lax.rem(z + oz, NZ), me), device_id_type=MESH)
    pl.semaphore_wait(barrier, len(peers) + NZ - 1)

    def coef_copy(ch, i):
        to = device_at(*peers[i])
        at = pl.ds(pl.multiple_of(to * rows + ch * CHUNK, NB), CHUNK)
        return pltpu.make_async_remote_copy(
            src_ref=coef_ref.at[:, at], dst_ref=panel.at[ch, me],
            send_sem=send_a.at[ch, i], recv_sem=recv_a.at[ch, i],
            device_id=(z, to), device_id_type=MESH,
        )

    def own_copy(ch):
        at = pl.ds(pl.multiple_of(me * rows + ch * CHUNK, NB), CHUNK)
        return pltpu.make_async_copy(coef_ref.at[:, at], panel.at[ch, me], local_a.at[ch])

    def start_chunk(ch, carry):
        own_copy(ch).start()
        for i in range(len(peers)):
            coef_copy(ch, i).start()
        return carry

    lax.fori_loop(0, chunks, start_chunk, 0)

    group = 4
    slots = idx_ref.shape[0]

    def build(step, carry):
        parts = [jnp.zeros((BLK, k), jnp.float32) for _ in range(group)]
        owners = [owner_ref[step * group + i] for i in range(group)]
        for t in range(slots):
            ids = jnp.broadcast_to(idx_ref[t:t + 1, :], (BLK, k))
            weights = w_ref[t]
            for i in range(group):
                parts[i] = parts[i] + jnp.where(ids == owners[i], weights, 0.0)
        at = pl.ds(pl.multiple_of(step * group * BLK, group * BLK), group * BLK)
        basis[at, :] = jnp.concatenate(parts, axis=0).astype(jnp.bfloat16)
        return carry

    lax.fori_loop(0, basis.shape[0] // (group * BLK), build, 0)

    gram[...] = jnp.zeros_like(gram)
    rhs[...] = jnp.zeros_like(rhs)

    def green_out(ch):
        at = pl.ds(pl.multiple_of(ch * CHUNK, CHUNK), CHUNK)
        return pltpu.make_async_copy(gbuf.at[at, :], green_ref.at[at, :], out_g.at[ch])

    def work_chunk(ch, carry):
        own_copy(ch).wait()
        for i in range(len(peers)):
            coef_copy(ch, i).wait_recv()
        block = panel[ch].reshape(NDEV * depth, CHUNK)
        green = dot_t(block, basis[...])
        row = lax.broadcasted_iota(jnp.int32, (CHUNK, k), 0) + ch * CHUNK
        green = jnp.where(row < live_ref[0], green, 0.0)
        at = pl.ds(pl.multiple_of(ch * CHUNK, CHUNK), CHUNK)
        gbuf[at, :] = green
        green_out(ch).start()
        high, low = split(green)
        gram[...] += dot_t(high, high) + (dot_t(high, low) + dot_t(low, high))
        line = jnp.broadcast_to(data_ref[:, at], (SB, CHUNK))
        column = jnp.transpose(line)[:, :1]
        rhs[...] += jnp.sum((green * column).reshape(CHUNK // SB, SB, k), axis=0)
        return carry

    lax.fori_loop(0, chunks, work_chunk, 0)

    blocks = upper_blocks(k)
    for i, (p, q) in enumerate(blocks):
        packed[i * NB:(i + 1) * NB, :] = gram[p * NB:(p + 1) * NB, q * NB:(q + 1) * NB]
    used = len(blocks) * NB
    packed[used:, :] = jnp.zeros((2 * HALF - used, NB), jnp.float32)
    rhs_row = jnp.sum(rhs[...], axis=0, keepdims=True)
    for i in range(k // NB):
        packed[used + i:used + i + 1, :] = rhs_row[:, i * NB:(i + 1) * NB]

    mine = pl.ds(pl.multiple_of(c * HALF, HALF), HALF)
    other = pl.ds(pl.multiple_of((1 - c) * HALF, HALF), HALF)
    core_copy = pltpu.make_async_remote_copy(
        src_ref=packed.at[other, :], dst_ref=from_core, send_sem=send_c, recv_sem=recv_c,
        device_id=(z, partner), device_id_type=MESH,
    )
    core_copy.start()
    core_copy.wait_recv()
    half[...] = packed[mine, :] + from_core[...]

    def chip_at(oy, ox):
        return lax.rem(y + oy, NY) * NX + lax.rem(x + ox, NX)

    def piece_copy(i):
        to = chip_at(*chips[i])
        return pltpu.make_async_remote_copy(
            src_ref=half.at[pl.ds(pl.multiple_of(to * PIECE, SB), PIECE), :], dst_ref=from_chip.at[i],
            send_sem=send_p.at[i], recv_sem=recv_p.at[i],
            device_id=(z, to * NC + c), device_id_type=MESH,
        )

    for i in range(len(chips)):
        piece_copy(i).start()
    part = half[pl.ds(pl.multiple_of(chip * PIECE, SB), PIECE), :]
    for i in reversed(range(len(chips))):
        piece_copy(i).wait_recv()
        part = part + from_chip[i]
    from_z[z] = part

    def z_copy(oz):
        return pltpu.make_async_remote_copy(
            src_ref=from_z.at[z], dst_ref=from_z.at[z], send_sem=send_z.at[oz - 1], recv_sem=recv_z.at[oz - 1],
            device_id=(lax.rem(z + oz, NZ), me), device_id_type=MESH,
        )

    for oz in (2, 1, 3):
        z_copy(oz).start()
    for oz in (1, 3, 2):
        z_copy(oz).wait_recv()

    def piece_of(chip_id):
        return pl.ds(pl.multiple_of(c * HALF + chip_id * PIECE, SB), PIECE)

    total[piece_of(chip), :] = (from_z[0] + from_z[1]) + (from_z[2] + from_z[3])

    def gather_copy(i):
        to = chip_at(*chips[i])
        return pltpu.make_async_remote_copy(
            src_ref=total.at[piece_of(chip), :], dst_ref=total.at[piece_of(chip), :],
            send_sem=send_g.at[i], recv_sem=recv_g.at[i],
            device_id=(z, to * NC + c), device_id_type=MESH,
        )

    def pass_on(chip_id, i):
        return pltpu.make_async_remote_copy(
            src_ref=total.at[piece_of(chip_id), :], dst_ref=total.at[piece_of(chip_id), :],
            send_sem=send_f.at[i], recv_sem=recv_f.at[i],
            device_id=(z, partner), device_id_type=MESH,
        )

    last = len(chips)
    for i in range(last):
        gather_copy(i).start()
    pass_on(chip, last).start()
    for i in reversed(range(last)):
        oy, ox = chips[i]
        gather_copy(i).wait_recv()
        pass_on(chip_at(NY - oy, NX - ox), i).start()
    for i in range(last + 1):
        pass_on(chip, i).wait()
    sum_ref[...] = total[...]

    core_copy.wait_send()
    for i in range(last):
        piece_copy(i).wait_send()
        gather_copy(i).wait_send()
    for oz in range(1, NZ):
        z_copy(oz).wait_send()

    def finish(ch, carry):
        green_out(ch).wait()
        for i in range(len(peers)):
            coef_copy(ch, i).wait_send()
        return carry

    lax.fori_loop(0, chunks, finish, 0)


def green_call(coef, basis_idx, basis_w, owner_blocks, data, panel_live):
    depth = coef.shape[0]
    rows = data.shape[0]
    k = basis_idx.shape[1]
    chunks = rows // CHUNK
    peers, chips = NDEV - 1, NCHIP - 1
    vmem = pl.BlockSpec(memory_space=pltpu.VMEM)
    smem = pl.BlockSpec(memory_space=pltpu.SMEM)
    anywhere = pl.BlockSpec(memory_space=pl.ANY)
    dma = pltpu.SemaphoreType.DMA
    f32 = jnp.float32
    return pl.pallas_call(
        green_kernel,
        out_shape=(jax.ShapeDtypeStruct((rows, k), f32), jax.ShapeDtypeStruct((2 * HALF, NB), f32)),
        in_specs=[smem, smem, anywhere, vmem, vmem, vmem],
        out_specs=(anywhere, vmem),
        scratch_shapes=[
            pltpu.VMEM((chunks, NDEV, depth, CHUNK), jnp.bfloat16),
            pltpu.VMEM((NDEV * depth, k), jnp.bfloat16),
            pltpu.VMEM((rows, k), f32),
            pltpu.VMEM((k, k), f32),
            pltpu.VMEM((SB, k), f32),
            pltpu.VMEM((2 * HALF, NB), f32),
            pltpu.VMEM((HALF, NB), f32),
            pltpu.VMEM((HALF, NB), f32),
            pltpu.VMEM((chips, PIECE, NB), f32),
            pltpu.VMEM((NZ, PIECE, NB), f32),
            pltpu.VMEM((2 * HALF, NB), f32),
            dma((chunks, peers)), dma((chunks, peers)), dma((chunks,)), dma((chunks,)),
            dma, dma, dma((chips,)), dma((chips,)), dma((NZ - 1,)), dma((NZ - 1,)),
            dma((chips,)), dma((chips,)), dma((chips + 1,)), dma((chips + 1,)),
        ],
        name="green",
        compiler_params=pltpu.CompilerParams(collective_id=0, has_side_effects=True, vmem_limit_bytes=56 << 20),
    )(owner_blocks, panel_live, coef, basis_idx, basis_w, data.reshape(1, rows))


def dot_hi(a, b, ca, cb):
    return lax.dot_general(a, b, (((ca,), (cb,)), ((), ())), precision=HI, preferred_element_type=jnp.float32)


def factor_block(d, v):
    n = len(d)
    sub = lax.broadcasted_iota(jnp.int32, (SB, NB), 0)

    def spread(part):
        return jnp.broadcast_to(part, (SB, NB))

    for g in range(n):
        j0 = SB * g
        cols = [spread(d[g][:, j0 + c:j0 + c + 1]) for c in range(SB)]
        invs, pd, pv, cross = [], [], [], []
        for c in range(SB):
            row = [None] * SB
            invs.append(1.0 / spread(cols[c][c:c + 1, :]))
            pd.append(spread(d[g][c:c + 1, :]))
            pv.append(spread(v[g][c:c + 1, :]))
            m = jnp.where(sub > c, cols[c] * invs[c], 0.0)
            for c2 in range(c + 1, SB):
                row[c2] = spread(cols[c2][c:c + 1, :])
                cols[c2] = cols[c2] - m * row[c2]
            cross.append(row)
            d[g] = d[g] - m * pd[c]
            v[g] = v[g] - m * pv[c]
        for i in range(g + 1, n):
            cols = [spread(d[i][:, j0 + c:j0 + c + 1]) for c in range(SB)]
            for c in range(SB):
                m = cols[c] * invs[c]
                for c2 in range(c + 1, SB):
                    cols[c2] = cols[c2] - m * cross[c][c2]
                d[i] = d[i] - m * pd[c]
                v[i] = v[i] - m * pv[c]
    return d, v


def factor_kernel(rows_total, tile, sum_ref, green_ref, r_ref, z_ref, q_ref, a, w, gbuf, qbuf, gsem, qsem):
    k = r_ref.shape[0]
    rows = green_ref.shape[0]
    nblk = k // NB
    get = pltpu.make_async_copy(green_ref, gbuf, gsem)
    get.start()
    a[...] = jnp.zeros_like(a)
    w[...] = jnp.zeros_like(w)
    blocks = upper_blocks(k)
    for i, (p, q) in enumerate(blocks):
        a[p * NB:(p + 1) * NB, q * NB:(q + 1) * NB] = sum_ref[i * NB:(i + 1) * NB, :]
    used = len(blocks) * NB
    rhs = jnp.concatenate([sum_ref[used + i:used + i + 1, :] for i in range(nblk)], axis=1)
    ri = lax.broadcasted_iota(jnp.int32, (NB, NB), 0)
    ci = lax.broadcasted_iota(jnp.int32, (NB, NB), 1)
    eye = jnp.where(ri == ci, 1.0, 0.0)
    for p in range(nblk):
        w[p * NB:(p + 1) * NB, p * NB:(p + 1) * NB] = eye

    def panel(p, carry):
        first = pl.multiple_of(p * NB, NB)
        at = pl.ds(first, NB)
        d = [a[pl.ds(first + SB * i, SB), at] for i in range(NB // SB)]
        v = [eye[SB * i:SB * i + SB] for i in range(NB // SB)]
        d, v = factor_block(d, v)
        dd = jnp.concatenate(d, axis=0)
        scale = lax.rsqrt(jnp.sum(jnp.where(ri == ci, dd, 0.0), axis=1, keepdims=True))
        vv = jnp.where(ri >= ci, jnp.concatenate(v, axis=0) * scale, 0.0)
        urow = dot_hi(vv, a[at, :], 1, 0)
        lane = lax.broadcasted_iota(jnp.int32, (NB, k), 1)
        urow = jnp.where(lane >= first + NB, urow, 0.0)
        a[at, :] = urow
        a[at, at] = jnp.where(ri <= ci, dd * scale, 0.0)
        wrow = dot_hi(vv, w[at, :], 1, 0)
        w[at, :] = wrow
        for q in range(1, nblk):
            @pl.when(q > p)
            def _():
                qs = slice(q * NB, (q + 1) * NB)
                u = a[at, qs]
                a[qs, :] = a[qs, :] - dot_hi(u, urow, 0, 0)
                w[qs, :] = w[qs, :] - dot_hi(u, wrow, 0, 0)
        return carry

    lax.fori_loop(0, nblk, panel, 0)
    for p in range(1, nblk):
        a[p * NB:(p + 1) * NB, :p * NB] = jnp.zeros((NB, p * NB), jnp.float32)
    r_ref[...] = a[...] * (1.0 / rows_total ** 0.5)
    z_ref[...] = dot_hi(rhs, w[...], 1, 1)
    inv_high, inv_low = split(w[...] * (rows_total ** 0.5))
    get.wait()

    def q_out(t):
        at = slice(t * tile, (t + 1) * tile)
        return pltpu.make_async_copy(qbuf.at[at, :], q_ref.at[at, :], qsem.at[t])

    def dot_n(left, right):
        return lax.dot_general(left, right, (((1,), (1,)), ((), ())), preferred_element_type=jnp.float32)

    for t in range(rows // tile):
        at = slice(t * tile, (t + 1) * tile)
        high, low = split(gbuf[at, :])
        qbuf[at, :] = dot_n(high, inv_high) + (dot_n(low, inv_high) + dot_n(high, inv_low))
        q_out(t).start()
    for t in range(rows // tile):
        q_out(t).wait()


def factor_call(gram_sum, green, rows_total):
    rows, k = green.shape
    tile = 512
    vmem = pl.BlockSpec(memory_space=pltpu.VMEM)
    anywhere = pl.BlockSpec(memory_space=pl.ANY)
    f32 = jnp.float32
    return pl.pallas_call(
        functools.partial(factor_kernel, rows_total, tile),
        out_shape=(jax.ShapeDtypeStruct((k, k), f32), jax.ShapeDtypeStruct((1, k), f32), jax.ShapeDtypeStruct((rows, k), f32)),
        in_specs=[vmem, anywhere],
        out_specs=(vmem, vmem, anywhere),
        scratch_shapes=[
            pltpu.VMEM((k, k), f32), pltpu.VMEM((k, k), f32),
            pltpu.VMEM((rows, k), f32), pltpu.VMEM((rows, k), f32),
            pltpu.SemaphoreType.DMA, pltpu.SemaphoreType.DMA((rows // tile,)),
        ],
        name="factor",
        compiler_params=pltpu.CompilerParams(vmem_limit_bytes=40 << 20),
    )(gram_sum, green)


def on_device(coef, basis_idx, basis_w, owner_blocks, data, panel_live):
    green, gram_sum = green_call(coef, basis_idx, basis_w, owner_blocks, data, panel_live)
    rows_total = green.shape[0] * lax.axis_size("dev") * lax.axis_size("grp")
    r_factor, projected, q_rows = factor_call(gram_sum, green, rows_total)
    return (r_factor, projected.reshape(-1), q_rows)


def solution(mesh):
    in_specs = (P("dev", "grp"), P(), P(), P(), P(("grp", "dev")), P(("grp", "dev")))
    out_specs = (P(), P(), P(("grp", "dev"), None))
    return jax.shard_map(
        on_device, mesh=mesh, in_specs=in_specs, out_specs=out_specs, check_vma=False
    )
```

time: 644 us -> 221 us (0.34); the launches traced: 634 us -> 219 us
  waiting for transfers between devices: 244 us -> 0 us
  Pallas kernels: 0 us -> 214 us
  other arithmetic: 176 us -> 0 us
  blocking collectives: 77.1 us -> 0 us
  matrix products: 62.4 us -> 0 us
  local copies, waits for them, and re-layouts: 49.1 us -> 3.91 us
  between operations: 18 us -> 1.46 us
  starting transfers between devices: 7.76 us -> 0 us
    pallas_call x0 -> x2, Pallas kernels: none -> 214 us  [the longest x1 182 us: green_call(): pl.pallas_call(green_kernel, out_shape=(jax.ShapeDtypeStruct((rows, k), f...]
    another operation x19 -> x0, other arithmetic: 172 us -> none  [the longest x14 90.7 us: on_device(): lower_factor = jnp.linalg.cholesky(gram_total)]
    all_to_all x1 -> x0, waiting for transfers between devices: 141 us -> none  [on_device(): lax.all_to_all(coef, 'dev', split_axis=1, concat_axis=0, tiled=True)]
    psum x2 -> x0, waiting for transfers between devices: 103 us -> none  [the longest x1 103 us: on_device(): gram_group, rhs_group = lax.psum((gram_local, rhs_local), 'dev')]
    psum x2 -> x0, blocking collectives: 77.1 us -> none  [the longest x1 66.2 us: on_device(): gram_group, rhs_group = lax.psum((gram_local, rhs_local), 'dev')]
    dot_general x4 -> x0, matrix products: 41.3 us -> none  [the longest x1 13.4 us: build_basis(): jnp.einsum('tbk,tdk->bdk', one_hot, basis_w, precision=lax.Precision.HIGH...]
    another operation x20 -> x0, matrix products: 21.1 us -> none  [the longest x7 15.2 us: on_device(): jax.scipy.linalg.solve_triangular(r_factor.T, green_rows.T, lower=True)]
    another operation x29 -> x0, local copies, waits for them, and re-layouts: 20.2 us -> none
  transfers between devices with their start and end apart: 3 -> 0, of which waited for: 2 -> 0; matrix products, arithmetic and copies ran while one was open for 4% -> 0% of each run, Pallas kernels for 0% -> 0%
where the time goes in v1:
time: 221 us; the launch traced here: 219 us
  Pallas kernels  214 us (97%)
  local copies, waits for them, and re-layouts  3.91 us (2%)
    pallas_call x1, Pallas kernels, green_call(): pl.pallas_call(green_kernel, out_shape=(jax.ShapeDtypeStruct((rows, k), f...  182 us
    pallas_call x1, Pallas kernels, factor_call(): pl.pallas_call(functools.partial(factor_kernel, rows_total, tile), out_sh...  31.8 us

profile of v1, /device:TPU:0, one launch (start us, length us, event | category | flops | bytes accessed | tf_op | source)
XLA Modules:
  0.0 219.2 jit_solution(15383715215794254062)
XLA Ops:
  1.3 182.1 %green.1 = (f32[3072,512]{1,0:T(8,128)}, f32[1536,128]{1,0:T(8,128)}) custom-call(s32[256]{0:T(256)} %owner_ref.1, s32[1]{0:T(128)S(6)} %copy.9.live_ref, bf16[64,98304]{1,0:T(8,128)(2,1)} %coef_ref.1, s32[64,512]{1,0:T(8,128)} %idx_ref.1, f32[64,8,512]{2,1,0:T(8,128)} %w_ref.1, f32[1,3072]{1,0:T(1,128)} %bitcast.2), custom_call_target="tpu_custom_call" | custom-call | tf_op jit(solution)/shard_map/green/pallas_call | solution.py:251
  183.4 0.0 copy-start
  183.4 2.8 %copy-done = f32[3072,512]{1,0:T(8,128)S(1)} copy-done((f32[3072,512]{1,0:T(8,128)S(1)}, f32[3072,512]{1,0:T(8,128)}, u32[]{:S(2)}) %copy-start) | copy-done | bytes 6291480
  186.2 0.0 copy-start.1
  186.2 1.1 copy-done.1
  187.3 31.8 %factor.1 = (f32[512,512]{1,0:T(8,128)}, f32[1,512]{1,0:T(1,128)}, f32[3072,512]{1,0:T(8,128)}) custom-call(f32[1536,128]{1,0:T(8,128)S(1)} %copy-done.1, f32[3072,512]{1,0:T(8,128)S(1)} %copy-done), custom_call_target="tpu_custom_call" | custom-call | tf_op jit(solution)/shard_map/factor/pallas_call | solution.py:389
Async XLA Ops:
  183.4 2.8 %copy-start = (f32[3072,512]{1,0:T(8,128)S(1)}, f32[3072,512]{1,0:T(8,128)}, u32[]{:S(2)}) copy-start(f32[3072,512]{1,0:T(8,128)} %get-tuple-element.9.green_ref) | copy-start | bytes 18874372
  186.2 1.1 copy-start.1

commit v2 on v1

--- a/solution.py
+++ b/solution.py
@@ -16,8 +16,10 @@
 NY, NX, NC, NZ = 4, 4, 2, 4
 NCHIP = NY * NX
 NDEV = NCHIP * NC
-PIECE = 48
+PIECE = 40
 HALF = NCHIP * PIECE
+RHS_AT = 120
+RHS_W = 64
 
 
 def hops(oy, ox):
@@ -49,9 +51,9 @@
 
 
 def green_kernel(
-    owner_ref, live_ref, coef_ref, idx_ref, w_ref, data_ref,
+    owner_ref, live_ref, coef_ref, idx_hbm, w_hbm, data_ref,
     green_ref, sum_ref,
-    panel, basis, gbuf, gram, rhs, packed, half, from_core, from_chip, from_z, total,
+    panel, basis, gbuf, idx_ref, w_ref, rhs, packed, half, from_core, from_chip, from_z, total, load,
     send_a, recv_a, local_a, out_g, send_c, recv_c, send_p, recv_p, send_z, recv_z, send_g, recv_g, send_f, recv_f,
 ):
     rows = green_ref.shape[0]
@@ -68,6 +70,10 @@
     def device_at(oy, ox, oc):
         return (lax.rem(y + oy, NY) * NX + lax.rem(x + ox, NX)) * NC + lax.rem(c + oc, NC)
 
+    loads = [pltpu.make_async_copy(idx_hbm, idx_ref, load.at[0]), pltpu.make_async_copy(w_hbm, w_ref, load.at[1])]
+    for one in loads:
+        one.start()
+
     barrier = pltpu.get_barrier_semaphore()
     for off in peers:
         pl.semaphore_signal(barrier, inc=1, device_id=(z, device_at(*off)), device_id_type=MESH)
@@ -111,9 +117,12 @@
         basis[at, :] = jnp.concatenate(parts, axis=0).astype(jnp.bfloat16)
         return carry
 
+    for one in loads:
+        one.wait()
     lax.fori_loop(0, basis.shape[0] // (group * BLK), build, 0)
 
-    gram[...] = jnp.zeros_like(gram)
+    blocks = upper_blocks(k)
+    packed[...] = jnp.zeros_like(packed)
     rhs[...] = jnp.zeros_like(rhs)
 
     def green_out(ch):
@@ -124,6 +133,12 @@
         own_copy(ch).wait()
         for i in range(len(peers)):
             coef_copy(ch, i).wait_recv()
+
+        @pl.when(ch > 0)
+        def _():
+            for i in range(len(peers)):
+                coef_copy(ch - 1, i).wait_send()
+
         block = panel[ch].reshape(NDEV * depth, CHUNK)
         green = dot_t(block, basis[...])
         row = lax.broadcasted_iota(jnp.int32, (CHUNK, k), 0) + ch * CHUNK
@@ -132,7 +147,9 @@
         gbuf[at, :] = green
         green_out(ch).start()
         high, low = split(green)
-        gram[...] += dot_t(high, high) + (dot_t(high, low) + dot_t(low, high))
+        gram = dot_t(high, high) + (dot_t(high, low) + dot_t(low, high))
+        for i, (p, q) in enumerate(blocks):
+            packed[i * NB:(i + 1) * NB, :] += gram[p * NB:(p + 1) * NB, q * NB:(q + 1) * NB]
         line = jnp.broadcast_to(data_ref[:, at], (SB, CHUNK))
         column = jnp.transpose(line)[:, :1]
         rhs[...] += jnp.sum((green * column).reshape(CHUNK // SB, SB, k), axis=0)
@@ -140,27 +157,23 @@
 
     lax.fori_loop(0, chunks, work_chunk, 0)
 
-    blocks = upper_blocks(k)
-    for i, (p, q) in enumerate(blocks):
-        packed[i * NB:(i + 1) * NB, :] = gram[p * NB:(p + 1) * NB, q * NB:(q + 1) * NB]
-    used = len(blocks) * NB
-    packed[used:, :] = jnp.zeros((2 * HALF - used, NB), jnp.float32)
     rhs_row = jnp.sum(rhs[...], axis=0, keepdims=True)
-    for i in range(k // NB):
-        packed[used + i:used + i + 1, :] = rhs_row[:, i * NB:(i + 1) * NB]
-
-    mine = pl.ds(pl.multiple_of(c * HALF, HALF), HALF)
-    other = pl.ds(pl.multiple_of((1 - c) * HALF, HALF), HALF)
-    core_copy = pltpu.make_async_remote_copy(
-        src_ref=packed.at[other, :], dst_ref=from_core, send_sem=send_c, recv_sem=recv_c,
-        device_id=(z, partner), device_id_type=MESH,
-    )
-    core_copy.start()
-    core_copy.wait_recv()
-    half[...] = packed[mine, :] + from_core[...]
+    for i in range(k // RHS_W):
+        packed[RHS_AT + i:RHS_AT + i + 1, :RHS_W] = rhs_row[:, i * RHS_W:(i + 1) * RHS_W]
 
     def chip_at(oy, ox):
         return lax.rem(y + oy, NY) * NX + lax.rem(x + ox, NX)
+
+    band = NX * PIECE
+
+    def core_copy(oy):
+        at = lax.rem(y + oy, NY) * band
+        return pltpu.make_async_remote_copy(
+            src_ref=packed.at[pl.ds(pl.multiple_of((1 - c) * HALF + at, SB), band), :],
+            dst_ref=from_core.at[pl.ds(pl.multiple_of(at, SB), band), :],
+            send_sem=send_c.at[oy], recv_sem=recv_c.at[oy],
+            device_id=(z, partner), device_id_type=MESH,
+        )
 
     def piece_copy(i):
         to = chip_at(*chips[i])
@@ -170,8 +183,17 @@
             device_id=(z, to * NC + c), device_id_type=MESH,
         )
 
-    for i in range(len(chips)):
-        piece_copy(i).start()
+    bands = (2, 1, 3, 0)
+    for oy in bands:
+        core_copy(oy).start()
+    for oy in bands:
+        core_copy(oy).wait_recv()
+        at = lax.rem(y + oy, NY) * band
+        here = pl.ds(pl.multiple_of(at, SB), band)
+        half[here, :] = packed[pl.ds(pl.multiple_of(c * HALF + at, SB), band), :] + from_core[here, :]
+        for i in range(len(chips)):
+            if chips[i][0] == oy:
+                piece_copy(i).start()
     part = half[pl.ds(pl.multiple_of(chip * PIECE, SB), PIECE), :]
     for i in reversed(range(len(chips))):
         piece_copy(i).wait_recv()
@@ -221,7 +243,8 @@
         pass_on(chip, i).wait()
     sum_ref[...] = total[...]
 
-    core_copy.wait_send()
+    for oy in bands:
+        core_copy(oy).wait_send()
     for i in range(last):
         piece_copy(i).wait_send()
         gather_copy(i).wait_send()
@@ -230,11 +253,11 @@
 
     def finish(ch, carry):
         green_out(ch).wait()
-        for i in range(len(peers)):
-            coef_copy(ch, i).wait_send()
         return carry
 
     lax.fori_loop(0, chunks, finish, 0)
+    for i in range(len(peers)):
+        coef_copy(chunks - 1, i).wait_send()
 
 
 def green_call(coef, basis_idx, basis_w, owner_blocks, data, panel_live):
@@ -251,13 +274,14 @@
     return pl.pallas_call(
         green_kernel,
         out_shape=(jax.ShapeDtypeStruct((rows, k), f32), jax.ShapeDtypeStruct((2 * HALF, NB), f32)),
-        in_specs=[smem, smem, anywhere, vmem, vmem, vmem],
+        in_specs=[smem, smem, anywhere, anywhere, anywhere, vmem],
         out_specs=(anywhere, vmem),
         scratch_shapes=[
             pltpu.VMEM((chunks, NDEV, depth, CHUNK), jnp.bfloat16),
             pltpu.VMEM((NDEV * depth, k), jnp.bfloat16),
             pltpu.VMEM((rows, k), f32),
-            pltpu.VMEM((k, k), f32),
+            pltpu.VMEM(basis_idx.shape, jnp.int32),
+            pltpu.VMEM(basis_w.shape, f32),
             pltpu.VMEM((SB, k), f32),
             pltpu.VMEM((2 * HALF, NB), f32),
             pltpu.VMEM((HALF, NB), f32),
@@ -265,8 +289,8 @@
             pltpu.VMEM((chips, PIECE, NB), f32),
             pltpu.VMEM((NZ, PIECE, NB), f32),
             pltpu.VMEM((2 * HALF, NB), f32),
-            dma((chunks, peers)), dma((chunks, peers)), dma((chunks,)), dma((chunks,)),
-            dma, dma, dma((chips,)), dma((chips,)), dma((NZ - 1,)), dma((NZ - 1,)),
+            dma((2,)), dma((chunks, peers)), dma((chunks, peers)), dma((chunks,)), dma((chunks,)),
+            dma((NY,)), dma((NY,)), dma((chips,)), dma((chips,)), dma((NZ - 1,)), dma((NZ - 1,)),
             dma((chips,)), dma((chips,)), dma((chips + 1,)), dma((chips + 1,)),
         ],
         name="green",
@@ -323,13 +347,12 @@
     blocks = upper_blocks(k)
     for i, (p, q) in enumerate(blocks):
         a[p * NB:(p + 1) * NB, q * NB:(q + 1) * NB] = sum_ref[i * NB:(i + 1) * NB, :]
-    used = len(blocks) * NB
-    rhs = jnp.concatenate([sum_ref[used + i:used + i + 1, :] for i in range(nblk)], axis=1)
+    rhs = jnp.concatenate([sum_ref[RHS_AT + i:RHS_AT + i + 1, :RHS_W] for i in range(k // RHS_W)], axis=1)
     ri = lax.broadcasted_iota(jnp.int32, (NB, NB), 0)
     ci = lax.broadcasted_iota(jnp.int32, (NB, NB), 1)
     eye = jnp.where(ri == ci, 1.0, 0.0)
-    for p in range(nblk):
-        w[p * NB:(p + 1) * NB, p * NB:(p + 1) * NB] = eye
+    corner = a[:NB, :NB]
+    a[:NB, :NB] = jnp.where((ri >= RHS_AT) & (ci < RHS_W), jnp.transpose(corner), corner)
 
     def panel(p, carry):
         first = pl.multiple_of(p * NB, NB)
@@ -339,21 +362,24 @@
         d, v = factor_block(d, v)
         dd = jnp.concatenate(d, axis=0)
         scale = lax.rsqrt(jnp.sum(jnp.where(ri == ci, dd, 0.0), axis=1, keepdims=True))
-        vv = jnp.where(ri >= ci, jnp.concatenate(v, axis=0) * scale, 0.0)
-        urow = dot_hi(vv, a[at, :], 1, 0)
-        lane = lax.broadcasted_iota(jnp.int32, (NB, k), 1)
-        urow = jnp.where(lane >= first + NB, urow, 0.0)
-        a[at, :] = urow
         a[at, at] = jnp.where(ri <= ci, dd * scale, 0.0)
-        wrow = dot_hi(vv, w[at, :], 1, 0)
-        w[at, :] = wrow
-        for q in range(1, nblk):
-            @pl.when(q > p)
+        w[at, at] = jnp.where(ri >= ci, jnp.concatenate(v, axis=0) * scale, 0.0)
+        for s in range(nblk):
+            @pl.when(p == s)
             def _():
-                qs = slice(q * NB, (q + 1) * NB)
-                u = a[at, qs]
-                a[qs, :] = a[qs, :] - dot_hi(u, urow, 0, 0)
-                w[qs, :] = w[qs, :] - dot_hi(u, wrow, 0, 0)
+                lo, hi = s * NB, (s + 1) * NB
+                inv = w[lo:hi, lo:hi]
+                right = k - hi
+                parts = ([a[lo:hi, hi:]] if right else []) + ([w[lo:hi, :lo]] if s else [])
+                line = dot_hi(inv, jnp.concatenate(parts, axis=1) if len(parts) > 1 else parts[0], 1, 0)
+                if s:
+                    w[lo:hi, :lo] = line[:, right:]
+                if right:
+                    u = line[:, :right]
+                    a[lo:hi, hi:] = u
+                    move = dot_hi(u, jnp.concatenate([line, inv], axis=1), 0, 0)
+                    a[hi:, hi:] = a[hi:, hi:] - move[:, :right]
+                    w[hi:, :hi] = w[hi:, :hi] - move[:, right:]
         return carry
 
     lax.fori_loop(0, nblk, panel, 0)
@@ -397,7 +423,7 @@
             pltpu.SemaphoreType.DMA, pltpu.SemaphoreType.DMA((rows // tile,)),
         ],
         name="factor",
-        compiler_params=pltpu.CompilerParams(vmem_limit_bytes=40 << 20),
+        compiler_params=pltpu.CompilerParams(vmem_limit_bytes=60 << 20),
     )(gram_sum, green)
 
 

time: 221 us -> 211 us (0.955)
  Pallas kernels: 214 us -> 208 us
  local copies, waits for them, and re-layouts: 3.91 us -> 0 us
    unnamed x4 -> x0, local copies, waits for them, and re-layouts: 3.91 us -> none
    pallas_call x1, Pallas kernels: 31.8 us -> 28.9 us  [factor_call(): pl.pallas_call(functools.partial(factor_kernel, rows_total, tile), out_sh...]
    pallas_call x1, Pallas kernels: 182 us -> 179 us  [green_call(): pl.pallas_call(green_kernel, out_shape=(jax.ShapeDtypeStruct((rows, k), f...]
where the time goes in v2:
time: 211 us; the launch traced here: 210 us
  Pallas kernels  208 us (99%)
    pallas_call x1, Pallas kernels, green_call(): pl.pallas_call(green_kernel, out_shape=(jax.ShapeDtypeStruct((rows, k), f...  179 us
    pallas_call x1, Pallas kernels, factor_call(): pl.pallas_call(functools.partial(factor_kernel, rows_total, tile), out_sh...  28.9 us

profile of v2, /device:TPU:0, one launch (start us, length us, event | category | flops | bytes accessed | tf_op | source)
XLA Modules:
  0.0 209.7 jit_solution(766551418876092432)
XLA Ops:
  1.3 179.4 %green.1 = (f32[3072,512]{1,0:T(8,128)}, f32[1280,128]{1,0:T(8,128)}) custom-call(s32[256]{0:T(256)} %owner_ref.1, s32[1]{0:T(128)S(6)} %copy.9.live_ref, bf16[64,98304]{1,0:T(8,128)(2,1)} %coef_ref.1, s32[64,512]{1,0:T(8,128)} %idx_hbm.1, f32[64,8,512]{2,1,0:T(8,128)} %w_hbm.1, f32[1,3072]{1,0:T(1,128)} %bitcast.2), custom_call_target="tpu_custom_call" | custom-call | tf_op jit(solution)/shard_map/green/pallas_call | solution.py:274
  180.7 28.9 %factor.1 = (f32[512,512]{1,0:T(8,128)}, f32[1,512]{1,0:T(1,128)}, f32[3072,512]{1,0:T(8,128)}) custom-call(f32[1280,128]{1,0:T(8,128)} %get-tuple-element.8.sum_ref, f32[3072,512]{1,0:T(8,128)} %get-tuple-element.9.green_ref), custom_call_target="tpu_custom_call" | custom-call | tf_op jit(solution)/shard_map/factor/pallas_call | solution.py:415

commit v3 on v2

--- a/solution.py
+++ b/solution.py
@@ -11,6 +11,7 @@
 MESH = pl.DeviceIdType.MESH
 NB = 128
 SB = 8
+STRIP = 8
 CHUNK = 256
 BLK = 8
 NY, NX, NC, NZ = 4, 4, 2, 4
@@ -302,37 +303,75 @@
     return lax.dot_general(a, b, (((ca,), (cb,)), ((), ())), precision=HI, preferred_element_type=jnp.float32)
 
 
+def dot_3(a, b, ca, cb):
+    a_high, a_low = split(a)
+    b_high, b_low = split(b)
+
+    def one(left, right):
+        return lax.dot_general(left, right, (((ca,), (cb,)), ((), ())), preferred_element_type=jnp.float32)
+
+    return one(a_high, b_high) + (one(a_low, b_high) + one(a_high, b_low))
+
+
 def factor_block(d, v):
     n = len(d)
     sub = lax.broadcasted_iota(jnp.int32, (SB, NB), 0)
 
-    def spread(part):
+    def bc(part):
         return jnp.broadcast_to(part, (SB, NB))
 
-    for g in range(n):
-        j0 = SB * g
-        cols = [spread(d[g][:, j0 + c:j0 + c + 1]) for c in range(SB)]
-        invs, pd, pv, cross = [], [], [], []
-        for c in range(SB):
-            row = [None] * SB
-            invs.append(1.0 / spread(cols[c][c:c + 1, :]))
-            pd.append(spread(d[g][c:c + 1, :]))
-            pv.append(spread(v[g][c:c + 1, :]))
-            m = jnp.where(sub > c, cols[c] * invs[c], 0.0)
-            for c2 in range(c + 1, SB):
-                row[c2] = spread(cols[c2][c:c + 1, :])
-                cols[c2] = cols[c2] - m * row[c2]
-            cross.append(row)
-            d[g] = d[g] - m * pd[c]
-            v[g] = v[g] - m * pv[c]
-        for i in range(g + 1, n):
-            cols = [spread(d[i][:, j0 + c:j0 + c + 1]) for c in range(SB)]
-            for c in range(SB):
-                m = cols[c] * invs[c]
-                for c2 in range(c + 1, SB):
-                    cols[c2] = cols[c2] - m * cross[c][c2]
-                d[i] = d[i] - m * pd[c]
-                v[i] = v[i] - m * pv[c]
+    for g0 in range(0, n, STRIP):
+        scaled = []
+        for g in range(g0, g0 + STRIP):
+            j0 = SB * g
+            def take(i):
+                return [bc(d[i][:, j0 + c:j0 + c + 1]) for c in range(SB)]
+            cols = take(g)
+            steps = []
+            iv = None
+            for c in range(0, SB, 2):
+                e = c + 1
+                first = [bc(cols[x][c:e, :]) for x in range(c, SB)]
+                second = [bc(cols[x][e:e + 1, :]) for x in range(e, SB)]
+                pa, pb, pc = first[0], first[1], second[0]
+                rdet = 1.0 / (pa * pc - pb * pb)
+                inva = 1.0 / pa
+                ka, kb, kc = pa * rdet, pb * rdet, pc * rdet
+                pd0, pd1 = bc(d[g][c:e, :]), bc(d[g][e:e + 1, :])
+                pv0, pv1 = bc(v[g][c:e, :]), bc(v[g][e:e + 1, :])
+                rest = ((first[x - c], second[x - e], x) for x in range(e + 1, SB))
+                step = (c, ka, kb, kc, list(rest), pd0, pd1, pv0, pv1)
+                steps.append(step)
+                u = cols[c] * kc - cols[e] * kb
+                t = cols[e] * ka - cols[c] * kb
+                u = jnp.where(sub > e, u, jnp.where(sub == e, pb * inva, 0.0))
+                t = jnp.where(sub > e, t, 0.0)
+                for f, s, x in step[4]:
+                    cols[x] = cols[x] - (u * f + t * s)
+                d[g] = d[g] - (u * pd0 + t * pd1)
+                v[g] = v[g] - (u * pv0 + t * pv1)
+                iv = inva if iv is None else jnp.where(sub == c, inva, iv)
+                iv = jnp.where(sub == e, ka, iv)
+            scaled.append(d[g] * iv)
+            for i in range(g + 1, g0 + STRIP):
+                cc = take(i)
+                for c, ka, kb, kc, rest, pd0, pd1, pv0, pv1 in steps:
+                    e = c + 1
+                    u = cc[c] * kc - cc[e] * kb
+                    t = cc[e] * ka - cc[c] * kb
+                    for f, s, x in rest:
+                        cc[x] = cc[x] - (u * f + t * s)
+                    d[i] = d[i] - (u * pd0 + t * pd1)
+                    v[i] = v[i] - (u * pv0 + t * pv1)
+        g1 = g0 + STRIP
+        if g1 < n:
+            left = jnp.concatenate(scaled, axis=0)[:, SB * g1:]
+            right = jnp.concatenate([jnp.concatenate(d[g0:g1], axis=0), jnp.concatenate(v[g0:g1], axis=0)], axis=1)
+            mv = dot_hi(left, right, 0, 0)
+            for i in range(g1, n):
+                o = SB * (i - g1)
+                d[i] = d[i] - mv[o:o + SB, :NB]
+                v[i] = v[i] - mv[o:o + SB, NB:]
     return d, v
 
 
@@ -371,13 +410,13 @@
                 inv = w[lo:hi, lo:hi]
                 right = k - hi
                 parts = ([a[lo:hi, hi:]] if right else []) + ([w[lo:hi, :lo]] if s else [])
-                line = dot_hi(inv, jnp.concatenate(parts, axis=1) if len(parts) > 1 else parts[0], 1, 0)
+                line = dot_3(inv, jnp.concatenate(parts, axis=1) if len(parts) > 1 else parts[0], 1, 0)
                 if s:
                     w[lo:hi, :lo] = line[:, right:]
                 if right:
                     u = line[:, :right]
                     a[lo:hi, hi:] = u
-                    move = dot_hi(u, jnp.concatenate([line, inv], axis=1), 0, 0)
+                    move = dot_3(u, jnp.concatenate([line, inv], axis=1), 0, 0)
                     a[hi:, hi:] = a[hi:, hi:] - move[:, :right]
                     w[hi:, :hi] = w[hi:, :hi] - move[:, right:]
         return carry
@@ -386,9 +425,7 @@
     for p in range(1, nblk):
         a[p * NB:(p + 1) * NB, :p * NB] = jnp.zeros((NB, p * NB), jnp.float32)
     r_ref[...] = a[...] * (1.0 / rows_total ** 0.5)
-    z_ref[...] = dot_hi(rhs, w[...], 1, 1)
     inv_high, inv_low = split(w[...] * (rows_total ** 0.5))
-    get.wait()
 
     def q_out(t):
         at = slice(t * tile, (t + 1) * tile)
@@ -397,10 +434,19 @@
     def dot_n(left, right):
         return lax.dot_general(left, right, (((1,), (1,)), ((), ())), preferred_element_type=jnp.float32)
 
+    wide = 2 * NB
+    rhs_high, rhs_low = split(jnp.broadcast_to(rhs, (SB, k)))
+    z = dot_n(rhs_high, inv_high) + (dot_n(rhs_low, inv_high) + dot_n(rhs_high, inv_low))
+    z_ref[...] = z[:1] * (1.0 / rows_total ** 0.5)
+    get.wait()
     for t in range(rows // tile):
         at = slice(t * tile, (t + 1) * tile)
         high, low = split(gbuf[at, :])
-        qbuf[at, :] = dot_n(high, inv_high) + (dot_n(low, inv_high) + dot_n(high, inv_low))
+        for n0 in range(0, k, wide):
+            n1 = n0 + wide
+            right_high, right_low = inv_high[n0:n1, :n1], inv_low[n0:n1, :n1]
+            left_high, left_low = high[:, :n1], low[:, :n1]
+            qbuf[at, n0:n1] = dot_n(left_high, right_high) + (dot_n(left_low, right_high) + dot_n(left_high, right_low))
         q_out(t).start()
     for t in range(rows // tile):
         q_out(t).wait()

time: 211 us -> 208 us (0.986)
  Pallas kernels: 208 us -> 205 us
    pallas_call x1, Pallas kernels: 28.9 us -> 25.4 us  [factor_call(): pl.pallas_call(functools.partial(factor_kernel, rows_total, tile), out_sh...]
where the time goes in v3:
time: 208 us; the launch traced here: 206 us
  Pallas kernels  205 us (99%)
    pallas_call x1, Pallas kernels, green_call(): pl.pallas_call(green_kernel, out_shape=(jax.ShapeDtypeStruct((rows, k), f...  179 us
    pallas_call x1, Pallas kernels, factor_call(): pl.pallas_call(functools.partial(factor_kernel, rows_total, tile), out_sh...  25.4 us

profile of v3, /device:TPU:0, one launch (start us, length us, event | category | flops | bytes accessed | tf_op | source)
XLA Modules:
  0.0 206.1 jit_solution(12408201963911828293)
XLA Ops:
  1.3 179.4 %green.1 = (f32[3072,512]{1,0:T(8,128)}, f32[1280,128]{1,0:T(8,128)}) custom-call(s32[256]{0:T(256)} %owner_ref.1, s32[1]{0:T(128)S(6)} %copy.9.live_ref, bf16[64,98304]{1,0:T(8,128)(2,1)} %coef_ref.1, s32[64,512]{1,0:T(8,128)} %idx_hbm.1, f32[64,8,512]{2,1,0:T(8,128)} %w_hbm.1, f32[1,3072]{1,0:T(1,128)} %bitcast.2), custom_call_target="tpu_custom_call" | custom-call | tf_op jit(solution)/shard_map/green/pallas_call | solution.py:275
  180.7 25.4 %factor.1 = (f32[512,512]{1,0:T(8,128)}, f32[1,512]{1,0:T(1,128)}, f32[3072,512]{1,0:T(8,128)}) custom-call(f32[1280,128]{1,0:T(8,128)} %get-tuple-element.8.sum_ref, f32[3072,512]{1,0:T(8,128)} %get-tuple-element.9.green_ref), custom_call_target="tpu_custom_call" | custom-call | tf_op jit(solution)/shard_map/factor/pallas_call | solution.py:461

commit v4 on v3

--- a/solution.py
+++ b/solution.py
@@ -76,7 +76,7 @@
         one.start()
 
     barrier = pltpu.get_barrier_semaphore()
-    for off in peers:
+    for off in reversed(peers):
         pl.semaphore_signal(barrier, inc=1, device_id=(z, device_at(*off)), device_id_type=MESH)
     for oz in range(1, NZ):
         pl.semaphore_signal(barrier, inc=1, device_id=(lax.rem(z + oz, NZ), me), device_id_type=MESH)
@@ -135,10 +135,12 @@
         for i in range(len(peers)):
             coef_copy(ch, i).wait_recv()
 
-        @pl.when(ch > 0)
+        @pl.when(ch < chunks - 1)
         def _():
-            for i in range(len(peers)):
-                coef_copy(ch - 1, i).wait_send()
+            @pl.when(ch > 0)
+            def _():
+                for i in range(len(peers)):
+                    coef_copy(ch - 1, i).wait_send()
 
         block = panel[ch].reshape(NDEV * depth, CHUNK)
         green = dot_t(block, basis[...])
@@ -187,6 +189,8 @@
     bands = (2, 1, 3, 0)
     for oy in bands:
         core_copy(oy).start()
+    for i in range(len(peers)):
+        coef_copy(chunks - 2, i).wait_send()
     for oy in bands:
         core_copy(oy).wait_recv()
         at = lax.rem(y + oy, NY) * band
@@ -195,6 +199,10 @@
         for i in range(len(chips)):
             if chips[i][0] == oy:
                 piece_copy(i).start()
+    for i in range(len(peers)):
+        coef_copy(chunks - 1, i).wait_send()
+    for oy in bands:
+        core_copy(oy).wait_send()
     part = half[pl.ds(pl.multiple_of(chip * PIECE, SB), PIECE), :]
     for i in reversed(range(len(chips))):
         piece_copy(i).wait_recv()
@@ -209,6 +217,14 @@
 
     for oz in (2, 1, 3):
         z_copy(oz).start()
+
+    def finish(ch, carry):
+        green_out(ch).wait()
+        return carry
+
+    lax.fori_loop(0, chunks, finish, 0)
+    for i in range(len(chips)):
+        piece_copy(i).wait_send()
     for oz in (1, 3, 2):
         z_copy(oz).wait_recv()
 
@@ -244,21 +260,10 @@
         pass_on(chip, i).wait()
     sum_ref[...] = total[...]
 
-    for oy in bands:
-        core_copy(oy).wait_send()
     for i in range(last):
-        piece_copy(i).wait_send()
         gather_copy(i).wait_send()
     for oz in range(1, NZ):
         z_copy(oz).wait_send()
-
-    def finish(ch, carry):
-        green_out(ch).wait()
-        return carry
-
-    lax.fori_loop(0, chunks, finish, 0)
-    for i in range(len(peers)):
-        coef_copy(chunks - 1, i).wait_send()
 
 
 def green_call(coef, basis_idx, basis_w, owner_blocks, data, panel_live):
@@ -375,23 +380,35 @@
     return d, v
 
 
-def factor_kernel(rows_total, tile, sum_ref, green_ref, r_ref, z_ref, q_ref, a, w, gbuf, qbuf, gsem, qsem):
+def factor_kernel(rows_total, tile, sum_ref, green_ref, r_ref, z_ref, q_ref, a, w, corner, gbuf, qbuf, bsem, gsem, qsem):
     k = r_ref.shape[0]
     rows = green_ref.shape[0]
     nblk = k // NB
+    blocks = upper_blocks(k)
+
+    def block_in(i):
+        p, q = blocks[i]
+        to = corner if i == 0 else a.at[p * NB:(p + 1) * NB, q * NB:(q + 1) * NB]
+        return pltpu.make_async_copy(sum_ref.at[i * NB:(i + 1) * NB, :], to, bsem.at[i])
+
+    for i in range(len(blocks)):
+        block_in(i).start()
     get = pltpu.make_async_copy(green_ref, gbuf, gsem)
     get.start()
-    a[...] = jnp.zeros_like(a)
+
+    def clear_lower():
+        for p in range(1, nblk):
+            a[p * NB:(p + 1) * NB, :p * NB] = jnp.zeros((NB, p * NB), jnp.float32)
+
+    clear_lower()
     w[...] = jnp.zeros_like(w)
-    blocks = upper_blocks(k)
-    for i, (p, q) in enumerate(blocks):
-        a[p * NB:(p + 1) * NB, q * NB:(q + 1) * NB] = sum_ref[i * NB:(i + 1) * NB, :]
-    rhs = jnp.concatenate([sum_ref[RHS_AT + i:RHS_AT + i + 1, :RHS_W] for i in range(k // RHS_W)], axis=1)
     ri = lax.broadcasted_iota(jnp.int32, (NB, NB), 0)
     ci = lax.broadcasted_iota(jnp.int32, (NB, NB), 1)
     eye = jnp.where(ri == ci, 1.0, 0.0)
-    corner = a[:NB, :NB]
-    a[:NB, :NB] = jnp.where((ri >= RHS_AT) & (ci < RHS_W), jnp.transpose(corner), corner)
+    block_in(0).wait()
+    head = corner[...]
+    rhs = jnp.concatenate([head[RHS_AT + i:RHS_AT + i + 1, :RHS_W] for i in range(k // RHS_W)], axis=1)
+    a[:NB, :NB] = jnp.where((ri >= RHS_AT) & (ci < RHS_W), jnp.transpose(head), head)
 
     def panel(p, carry):
         first = pl.multiple_of(p * NB, NB)
@@ -406,6 +423,9 @@
         for s in range(nblk):
             @pl.when(p == s)
             def _():
+                if s == 0:
+                    for i in range(1, len(blocks)):
+                        block_in(i).wait()
                 lo, hi = s * NB, (s + 1) * NB
                 inv = w[lo:hi, lo:hi]
                 right = k - hi
@@ -422,8 +442,7 @@
         return carry
 
     lax.fori_loop(0, nblk, panel, 0)
-    for p in range(1, nblk):
-        a[p * NB:(p + 1) * NB, :p * NB] = jnp.zeros((NB, p * NB), jnp.float32)
+    clear_lower()
     r_ref[...] = a[...] * (1.0 / rows_total ** 0.5)
     inv_high, inv_low = split(w[...] * (rows_total ** 0.5))
 
@@ -461,12 +480,12 @@
     return pl.pallas_call(
         functools.partial(factor_kernel, rows_total, tile),
         out_shape=(jax.ShapeDtypeStruct((k, k), f32), jax.ShapeDtypeStruct((1, k), f32), jax.ShapeDtypeStruct((rows, k), f32)),
-        in_specs=[vmem, anywhere],
+        in_specs=[anywhere, anywhere],
         out_specs=(vmem, vmem, anywhere),
         scratch_shapes=[
-            pltpu.VMEM((k, k), f32), pltpu.VMEM((k, k), f32),
+            pltpu.VMEM((k, k), f32), pltpu.VMEM((k, k), f32), pltpu.VMEM((NB, NB), f32),
             pltpu.VMEM((rows, k), f32), pltpu.VMEM((rows, k), f32),
-            pltpu.SemaphoreType.DMA, pltpu.SemaphoreType.DMA((rows // tile,)),
+            pltpu.SemaphoreType.DMA((len(upper_blocks(k)),)), pltpu.SemaphoreType.DMA, pltpu.SemaphoreType.DMA((rows // tile,)),
         ],
         name="factor",
         compiler_params=pltpu.CompilerParams(vmem_limit_bytes=60 << 20),

time: 208 us -> 206 us (level)
  no operation moved by 1% of the time
where the time goes in v4:
time: 206 us; the launch traced here: 205 us
  Pallas kernels  203 us (99%)
    pallas_call x1, Pallas kernels, green_call(): pl.pallas_call(green_kernel, out_shape=(jax.ShapeDtypeStruct((rows, k), f...  178 us
    pallas_call x1, Pallas kernels, factor_call(): pl.pallas_call(functools.partial(factor_kernel, rows_total, tile), out_sh...  25.2 us

profile of v4, /device:TPU:0, one launch (start us, length us, event | category | flops | bytes accessed | tf_op | source)
XLA Modules:
  0.0 204.7 jit_solution(16564208666248667433)
XLA Ops:
  1.3 178.2 %green.1 = (f32[3072,512]{1,0:T(8,128)}, f32[1280,128]{1,0:T(8,128)}) custom-call(s32[256]{0:T(256)} %owner_ref.1, s32[1]{0:T(128)S(6)} %copy.9.live_ref, bf16[64,98304]{1,0:T(8,128)(2,1)} %coef_ref.1, s32[64,512]{1,0:T(8,128)} %idx_hbm.1, f32[64,8,512]{2,1,0:T(8,128)} %w_hbm.1, f32[1,3072]{1,0:T(1,128)} %bitcast.2), custom_call_target="tpu_custom_call" | custom-call | tf_op jit(solution)/shard_map/green/pallas_call | solution.py:280
  179.5 25.2 %factor.1 = (f32[512,512]{1,0:T(8,128)}, f32[1,512]{1,0:T(1,128)}, f32[3072,512]{1,0:T(8,128)}) custom-call(f32[1280,128]{1,0:T(8,128)} %get-tuple-element.8.sum_ref, f32[3072,512]{1,0:T(8,128)} %get-tuple-element.9.green_ref), custom_call_target="tpu_custom_call" | custom-call | tf_op jit(solution)/shard_map/factor/pallas_call | solution.py:480

commit v5 on v4

--- a/solution.py
+++ b/solution.py
@@ -52,9 +52,9 @@
 
 
 def green_kernel(
-    owner_ref, live_ref, coef_ref, idx_hbm, w_hbm, data_ref,
+    owner_hbm, live_ref, coef_ref, idx_hbm, w_hbm, data_hbm,
     green_ref, sum_ref,
-    panel, basis, gbuf, idx_ref, w_ref, rhs, packed, half, from_core, from_chip, from_z, total, load,
+    panel, basis, gbuf, owner_ref, idx_ref, w_ref, data_ref, rhs, packed, half, from_core, from_chip, from_z, total, load,
     send_a, recv_a, local_a, out_g, send_c, recv_c, send_p, recv_p, send_z, recv_z, send_g, recv_g, send_f, recv_f,
 ):
     rows = green_ref.shape[0]
@@ -71,7 +71,8 @@
     def device_at(oy, ox, oc):
         return (lax.rem(y + oy, NY) * NX + lax.rem(x + ox, NX)) * NC + lax.rem(c + oc, NC)
 
-    loads = [pltpu.make_async_copy(idx_hbm, idx_ref, load.at[0]), pltpu.make_async_copy(w_hbm, w_ref, load.at[1])]
+    pairs = ((idx_hbm, idx_ref), (w_hbm, w_ref), (data_hbm, data_ref), (owner_hbm, owner_ref))
+    loads = [pltpu.make_async_copy(src, dst, load.at[i]) for i, (src, dst) in enumerate(pairs)]
     for one in loads:
         one.start()
 
@@ -147,8 +148,6 @@
         row = lax.broadcasted_iota(jnp.int32, (CHUNK, k), 0) + ch * CHUNK
         green = jnp.where(row < live_ref[0], green, 0.0)
         at = pl.ds(pl.multiple_of(ch * CHUNK, CHUNK), CHUNK)
-        gbuf[at, :] = green
-        green_out(ch).start()
         high, low = split(green)
         gram = dot_t(high, high) + (dot_t(high, low) + dot_t(low, high))
         for i, (p, q) in enumerate(blocks):
@@ -156,6 +155,8 @@
         line = jnp.broadcast_to(data_ref[:, at], (SB, CHUNK))
         column = jnp.transpose(line)[:, :1]
         rhs[...] += jnp.sum((green * column).reshape(CHUNK // SB, SB, k), axis=0)
+        gbuf[at, :] = green
+        green_out(ch).start()
         return carry
 
     lax.fori_loop(0, chunks, work_chunk, 0)
@@ -280,14 +281,16 @@
     return pl.pallas_call(
         green_kernel,
         out_shape=(jax.ShapeDtypeStruct((rows, k), f32), jax.ShapeDtypeStruct((2 * HALF, NB), f32)),
-        in_specs=[smem, smem, anywhere, anywhere, anywhere, vmem],
+        in_specs=[anywhere, smem, anywhere, anywhere, anywhere, anywhere],
         out_specs=(anywhere, vmem),
         scratch_shapes=[
             pltpu.VMEM((chunks, NDEV, depth, CHUNK), jnp.bfloat16),
             pltpu.VMEM((NDEV * depth, k), jnp.bfloat16),
             pltpu.VMEM((rows, k), f32),
+            pltpu.SMEM(owner_blocks.shape, jnp.int32),
             pltpu.VMEM(basis_idx.shape, jnp.int32),
             pltpu.VMEM(basis_w.shape, f32),
+            pltpu.VMEM((1, rows), f32),
             pltpu.VMEM((SB, k), f32),
             pltpu.VMEM((2 * HALF, NB), f32),
             pltpu.VMEM((HALF, NB), f32),
@@ -295,7 +298,7 @@
             pltpu.VMEM((chips, PIECE, NB), f32),
             pltpu.VMEM((NZ, PIECE, NB), f32),
             pltpu.VMEM((2 * HALF, NB), f32),
-            dma((2,)), dma((chunks, peers)), dma((chunks, peers)), dma((chunks,)), dma((chunks,)),
+            dma((4,)), dma((chunks, peers)), dma((chunks, peers)), dma((chunks,)), dma((chunks,)),
             dma((NY,)), dma((NY,)), dma((chips,)), dma((chips,)), dma((NZ - 1,)), dma((NZ - 1,)),
             dma((chips,)), dma((chips,)), dma((chips + 1,)), dma((chips + 1,)),
         ],

time: 206 us -> 205 us (level)
  no operation moved by 1% of the time
where the time goes in v5:
time: 205 us; the launch traced here: 204 us
  Pallas kernels  203 us (99%)
    pallas_call x1, Pallas kernels, green_call(): pl.pallas_call(green_kernel, out_shape=(jax.ShapeDtypeStruct((rows, k), f...  178 us
    pallas_call x1, Pallas kernels, factor_call(): pl.pallas_call(functools.partial(factor_kernel, rows_total, tile), out_sh...  25.2 us

profile of v5, /device:TPU:0, one launch (start us, length us, event | category | flops | bytes accessed | tf_op | source)
XLA Modules:
  0.0 204.0 jit_solution(13169430319255007655)
XLA Ops:
  1.3 177.5 %green.1 = (f32[3072,512]{1,0:T(8,128)}, f32[1280,128]{1,0:T(8,128)}) custom-call(s32[256]{0:T(256)} %owner_hbm.1, s32[1]{0:T(128)S(6)} %copy.9.live_ref, bf16[64,98304]{1,0:T(8,128)(2,1)} %coef_ref.1, s32[64,512]{1,0:T(8,128)} %idx_hbm.1, f32[64,8,512]{2,1,0:T(8,128)} %w_hbm.1, f32[1,3072]{1,0:T(1,128)} %bitcast.2), custom_call_target="tpu_custom_call" | custom-call | tf_op jit(solution)/shard_map/green/pallas_call | solution.py:281
  178.8 25.2 %factor.1 = (f32[512,512]{1,0:T(8,128)}, f32[1,512]{1,0:T(1,128)}, f32[3072,512]{1,0:T(8,128)}) custom-call(f32[1280,128]{1,0:T(8,128)} %get-tuple-element.8.sum_ref, f32[3072,512]{1,0:T(8,128)} %get-tuple-element.9.green_ref), custom_call_target="tpu_custom_call" | custom-call | tf_op jit(solution)/shard_map/factor/pallas_call | solution.py:483
